TPU v7x, 32 devices: a whole 2x2x4 slice. The times are simulated.
32 devices in a mesh: tensor: 2 (over x), expert: 8 (over z, y), replica: 2 (over core).
Axes of the slice: x: 2, y: 2, z: 4, core: 2. Of those that a mesh axis runs over, the one named last changes fastest.
Arguments:
- tokens: bfloat16 [6304, 768], P(('expert', 'replica')), may hold values from -6 to 6
- gains: float32 [2, 2, 768], replicated, may hold values from 0.5 to 1.5
- attn_qkv: bfloat16 [2, 3, 768, 768], P(None, None, None, 'tensor'), may hold values from -0.21875 to 0.21875
- attn_out: bfloat16 [2, 768, 768], P(None, 'tensor'), may hold values from -3 to 3
- router: bfloat16 [2, 768, 8], replicated, may hold values from -0.15625 to 0.15625
- expert_in: bfloat16 [2, 8, 768, 3072], P(None, 'expert', None, 'tensor'), may hold values from -0.21875 to 0.21875
- expert_out: bfloat16 [2, 8, 3072, 768], P(None, 'expert', 'tensor'), may hold values from -1.75 to 1.75
- routes: int32 [2, 6304, 2], P(None, ('expert', 'replica')), may hold values from 0 to 7, all different within a row; in each aligned block of 394 rows (0 to 393, 394 to 787, ..., all dimensions but the last counted through in order) at most 128 rows name the same one
- cotangent: bfloat16 [6304, 768], P(('expert', 'replica')), may hold values from -6 to 6
Outputs:
- mixed_out: bfloat16 [6304, 768], P(('expert', 'replica'))
- grad_tokens: float32 [6304, 768], P(('expert', 'replica'))
- grad_gains: float32 [2, 2, 768], replicated
- grad_attn_qkv: float32 [2, 3, 768, 768], P(None, None, None, 'tensor')
- grad_attn_out: float32 [2, 768, 768], P(None, 'tensor')
- grad_router: float32 [2, 768, 8], replicated
- grad_expert_in: float32 [2, 8, 768, 3072], P(None, 'expert', 'replica', 'tensor')
- grad_expert_out: float32 [2, 8, 3072, 768], P(None, 'expert', 'tensor', 'replica')
Inputs may be any that keep to these rules, and one draw needn't show every extreme that they name: In the tokens of one block of 394, no expert is named by more than 128 routes, and in every draw some expert by exactly 128; the two experts of a token differ.
All inputs are finite; a program needn't handle non-finite values.
Results may differ from a plain program's by a relative error of at most 0.02.
Values may be sent and summed in bfloat16 or wider, within the bound.
No kernel may reach another device: no remote copies, remote signals or barrier semaphores. Data moves between devices by JAX's collectives and lax.ppermute only.
A program may use at most 192 MiB of HBM per device.

v0:
```python
import jax
import jax.numpy as jnp
from jax import lax
from jax.sharding import PartitionSpec as P

HEAD_DIM = 64
SEQ = 197
EPSILON = 1e-06


def layer_norm(stream, gain):
    center = jnp.mean(stream, axis=-1, keepdims=True)
    shifted = stream - center
    spread = jnp.mean(shifted * shifted, axis=-1, keepdims=True)
    return shifted * lax.rsqrt(spread + EPSILON) * gain


def slot_index(route_ids, expert_count, capacity):
    labels = lax.broadcasted_iota(jnp.int32, (1, 1, expert_count), 2)
    route_hits = jnp.sum((route_ids[:, :, None] == labels).astype(jnp.int32), axis=1)
    before = jnp.cumsum(route_hits, axis=0) - route_hits
    return route_ids * capacity + jnp.take_along_axis(before, route_ids, axis=1)


def on_device(tokens, gains, attn_qkv, attn_out, router, expert_in, expert_out, routes, cotangent):
    row_count, model_width = tokens.shape
    layer_count = attn_qkv.shape[0]
    local_width = attn_qkv.shape[3]
    local_heads = local_width // HEAD_DIM
    image_count = row_count // SEQ
    expert_count = router.shape[2]
    capacity = 8 * (5 * row_count // (16 * expert_count) + 1)
    score_scale = HEAD_DIM ** (-0.5)
    residual = tokens.astype(jnp.float32)
    saved = []
    for layer_index in range(layer_count):
        normed, norm_pull = jax.vjp(layer_norm, residual, gains[layer_index, 0])
        normed_bf = normed.astype(jnp.bfloat16)
        projected = jnp.einsum(
            "td,cdf->ctf", normed_bf, attn_qkv[layer_index], preferred_element_type=jnp.float32
        ).astype(jnp.bfloat16)
        head_view = projected.reshape(3, image_count, SEQ, local_heads, HEAD_DIM)
        scores = (
            jnp.einsum(
                "bqhe,bkhe->bhqk", head_view[0], head_view[1], preferred_element_type=jnp.float32
            )
            * score_scale
        )
        row_max = jnp.max(scores, axis=-1, keepdims=True)
        exp_scores = jnp.exp(scores - row_max)
        exp_total = jnp.sum(exp_scores, axis=-1, keepdims=True)
        log_total = row_max + jnp.log(exp_total)
        attn_probs = (exp_scores / exp_total).astype(jnp.bfloat16)
        mixed_rows = jnp.einsum(
            "bhqk,bkhe->bqhe", attn_probs, head_view[2], preferred_element_type=jnp.float32
        )
        mixed_rows = mixed_rows.reshape(row_count, local_width).astype(jnp.bfloat16)
        attn_part = jnp.dot(mixed_rows, attn_out[layer_index], preferred_element_type=jnp.float32)
        residual = residual + lax.psum(attn_part, "tensor")
        moe_in, moe_pull = jax.vjp(layer_norm, residual, gains[layer_index, 1])
        moe_bf = moe_in.astype(jnp.bfloat16)
        gate_probs = jax.nn.softmax(
            jnp.dot(moe_bf, router[layer_index], preferred_element_type=jnp.float32), axis=-1
        )
        route_ids = routes[layer_index]
        slot_rows = slot_index(route_ids, expert_count, capacity).reshape(-1)
        picked = jnp.take_along_axis(gate_probs, route_ids, axis=1)
        send_buffer = jnp.zeros((expert_count * capacity, model_width), jnp.bfloat16)
        send_buffer = (
            send_buffer.at[slot_rows]
            .set(jnp.repeat(moe_bf, 2, axis=0))
            .reshape(expert_count, capacity, model_width)
        )
        received = lax.all_to_all(send_buffer, "expert", split_axis=0, concat_axis=0, tiled=True)
        source_count = received.shape[0]
        flat_in = received.reshape(-1, model_width)
        pre_act = jnp.dot(flat_in, expert_in[layer_index, 0], preferred_element_type=jnp.float32)
        activation = jax.nn.gelu(pre_act).astype(jnp.bfloat16)
        expert_part = jnp.dot(
            activation, expert_out[layer_index, 0], preferred_element_type=jnp.float32
        )
        expert_part = expert_part.reshape(source_count, capacity, model_width)
        returned = lax.all_to_all(expert_part, "expert", split_axis=0, concat_axis=0, tiled=True)
        chosen = returned.reshape(-1, model_width)[slot_rows].reshape(row_count, 2, model_width)
        moe_part = jnp.sum(picked[:, :, None] * chosen, axis=1)
        residual = residual + lax.psum(moe_part, "tensor")
        kept_act = pre_act
        saved.append(
            (
                normed_bf,
                norm_pull,
                head_view,
                log_total,
                mixed_rows,
                moe_bf,
                moe_pull,
                gate_probs,
                route_ids,
                slot_rows,
                picked,
                received,
                kept_act,
                chosen,
            )
        )
    mixed_out = residual.astype(jnp.bfloat16)
    upstream = cotangent.astype(jnp.float32)
    raw_grads = [None] * layer_count
    labels = lax.broadcasted_iota(jnp.int32, (1, 1, expert_count), 2)
    for layer_index in reversed(range(layer_count)):
        (
            normed_bf,
            norm_pull,
            head_view,
            log_total,
            mixed_rows,
            moe_bf,
            moe_pull,
            gate_probs,
            route_ids,
            slot_rows,
            picked,
            received,
            kept_act,
            chosen,
        ) = saved[layer_index]
        slot_grad = (
            (picked[:, :, None] * upstream[:, None, :])
            .astype(jnp.bfloat16)
            .reshape(-1, model_width)
        )
        grad_send = jnp.zeros((expert_count * capacity, model_width), jnp.bfloat16)
        grad_send = (
            grad_send.at[slot_rows].set(slot_grad).reshape(expert_count, capacity, model_width)
        )
        grad_recv = lax.all_to_all(grad_send, "expert", split_axis=0, concat_axis=0, tiled=True)
        source_count = grad_recv.shape[0]
        grad_recv = grad_recv.reshape(-1, model_width)
        flat_in = received.reshape(-1, model_width)
        pre_act = kept_act
        activation, gelu_pull = jax.vjp(jax.nn.gelu, pre_act)
        act_grad = jnp.einsum(
            "sd,fd->sf", grad_recv, expert_out[layer_index, 0], preferred_element_type=jnp.float32
        )
        pre_grad = gelu_pull(act_grad)[0].astype(jnp.bfloat16)
        grad_w_out = jnp.einsum(
            "sf,sd->fd",
            activation.astype(jnp.bfloat16),
            grad_recv,
            preferred_element_type=jnp.float32,
        )
        grad_w_in = jnp.einsum("sd,sf->df", flat_in, pre_grad, preferred_element_type=jnp.float32)
        input_grad = jnp.einsum(
            "sf,df->sd", pre_grad, expert_in[layer_index, 0], preferred_element_type=jnp.float32
        )
        input_grad = input_grad.reshape(source_count, capacity, model_width)
        home_grad = lax.all_to_all(input_grad, "expert", split_axis=0, concat_axis=0, tiled=True)
        row_grad = jnp.sum(
            home_grad.reshape(-1, model_width)[slot_rows].reshape(row_count, 2, model_width), axis=1
        )
        gate_dot = jnp.sum(upstream[:, None, :] * chosen, axis=-1)
        row_grad, gate_dot = lax.psum((row_grad, gate_dot), "tensor")
        prob_grad = jnp.sum(
            gate_dot[:, :, None] * (route_ids[:, :, None] == labels).astype(jnp.float32), axis=1
        )
        logit_grad = gate_probs * (
            prob_grad - jnp.sum(prob_grad * gate_probs, axis=-1, keepdims=True)
        )
        logit_grad = logit_grad.astype(jnp.bfloat16)
        grad_router = jnp.einsum(
            "td,te->de", moe_bf, logit_grad, preferred_element_type=jnp.float32
        )
        norm_grad = row_grad + jnp.einsum(
            "te,de->td", logit_grad, router[layer_index], preferred_element_type=jnp.float32
        )
        resid_grad, gain_two = moe_pull(norm_grad)
        upstream = upstream + resid_grad
        out_grad = upstream.astype(jnp.bfloat16)
        grad_attn_out = jnp.einsum(
            "tf,td->fd", mixed_rows, out_grad, preferred_element_type=jnp.float32
        )
        mixed_grad = jnp.einsum(
            "td,fd->tf", out_grad, attn_out[layer_index], preferred_element_type=jnp.float32
        )
        mixed_grad = mixed_grad.astype(jnp.bfloat16).reshape(
            image_count, SEQ, local_heads, HEAD_DIM
        )
        scores = (
            jnp.einsum(
                "bqhe,bkhe->bhqk", head_view[0], head_view[1], preferred_element_type=jnp.float32
            )
            * score_scale
        )
        attn_probs = jnp.exp(scores - log_total)
        value_grad = jnp.einsum(
            "bhqk,bqhe->bkhe",
            attn_probs.astype(jnp.bfloat16),
            mixed_grad,
            preferred_element_type=jnp.float32,
        )
        prob_grad = jnp.einsum(
            "bqhe,bkhe->bhqk", mixed_grad, head_view[2], preferred_element_type=jnp.float32
        )
        score_grad = attn_probs * (
            prob_grad - jnp.sum(prob_grad * attn_probs, axis=-1, keepdims=True)
        )
        score_grad = score_grad.astype(jnp.bfloat16)
        query_grad = (
            jnp.einsum(
                "bhqk,bkhe->bqhe", score_grad, head_view[1], preferred_element_type=jnp.float32
            )
            * score_scale
        )
        key_grad = (
            jnp.einsum(
                "bhqk,bqhe->bkhe", score_grad, head_view[0], preferred_element_type=jnp.float32
            )
            * score_scale
        )
        proj_grad = (
            jnp.stack([query_grad, key_grad, value_grad])
            .reshape(3, row_count, local_width)
            .astype(jnp.bfloat16)
        )
        grad_qkv = jnp.einsum(
            "td,ctf->cdf", normed_bf, proj_grad, preferred_element_type=jnp.float32
        )
        norm_grad = jnp.einsum(
            "ctf,cdf->td", proj_grad, attn_qkv[layer_index], preferred_element_type=jnp.float32
        )
        norm_grad = lax.psum(norm_grad, "tensor")
        resid_grad, gain_one = norm_pull(norm_grad)
        upstream = upstream + resid_grad
        gain_pair = jnp.stack([gain_one, gain_two])
        raw_grads[layer_index] = (
            grad_w_in,
            grad_w_out,
            grad_qkv,
            grad_attn_out,
            grad_router,
            gain_pair,
        )
    stacked = [jnp.stack([item[position] for item in raw_grads]) for position in range(6)]
    grad_in_all, grad_out_all = (
        lax.psum_scatter(stacked[0], "replica", scatter_dimension=1, tiled=True),
        lax.psum_scatter(stacked[1], "replica", scatter_dimension=2, tiled=True),
    )
    grad_qkv_all, grad_proj_all, grad_router_all, grad_gain_all = lax.psum(
        (stacked[2], stacked[3], stacked[4], stacked[5]), ("expert", "replica")
    )
    return (
        mixed_out,
        upstream,
        grad_gain_all,
        grad_qkv_all,
        grad_proj_all,
        grad_router_all,
        grad_in_all[:, None],
        grad_out_all[:, None],
    )


def solution(mesh):
    return jax.shard_map(
        on_device,
        mesh=mesh,
        in_specs=(
            P(("expert", "replica"), None),
            P(),
            P(None, None, None, "tensor"),
            P(None, "tensor", None),
            P(),
            P(None, "expert", None, "tensor"),
            P(None, "expert", "tensor", None),
            P(None, ("expert", "replica"), None),
            P(("expert", "replica"), None),
        ),
        out_specs=(
            P(("expert", "replica"), None),
            P(("expert", "replica"), None),
            P(),
            P(None, None, None, "tensor"),
            P(None, "tensor", None),
            P(),
            P(None, "expert", "replica", "tensor"),
            P(None, "expert", "tensor", "replica"),
        ),
        check_vma=False,
    )
```

profile of v0, /device:TPU:0, one launch (start us, length us, event | category | flops | bytes accessed | tf_op | source)
XLA Modules:
  0.0 1209.6 jit_solution(15359523138905654827)
XLA Ops:
  24.5 8.1 gather_fusion.5
  33.1 35.5 %all-reduce.14.cloned.1.call-done = f32[394,768]{1,0:T(8,128)} async-done(((f32[394,768]{1,0:T(8,128)}), f32[394,768]{1,0:T(8,128)}) %all-reduce.14.cloned.1.call-update) | async-done | bytes 1210384 | tf_op jit(solution)/shard_map/psum | solution.py:59
  73.3 6.1 scatter_custom_fusion
  79.4 42.6 %all_to_all.40 = bf16[8,128,768]{2,1,0:T(8,128)(2,1)S(1)} all-to-all(bf16[8,128,768]{2,1,0:T(8,128)(2,1)S(1)} %bitcast.271), channel_id=1, replica_groups=mesh['tensor'=2,'expert'=8,'replica'=2] {'expert'}, dimensions={0} | all-to-all | bytes 3145728 | tf_op jit(solution)/shard_map/all_to_all | solution.py:74
  122.0 7.6 multiply_convert_fusion.1
  129.6 4.3 fusion.20
  133.9 3.8 all-to-all-start.1
  139.7 8.3 gather_fusion.4
  150.6 57.4 %all-to-all-done.1 = f32[8,128,768]{2,1,0:T(8,128)S(1)} async-done(((f32[8,128,768]{2,1,0:T(8,128)}), f32[8,128,768]{2,1,0:T(8,128)S(1)}, u32[]{:S(2)}, u32[]{:S(2)}) %all-to-all-start.1) | async-done | bytes 3145760 | tf_op jit(solution)/shard_map/all_to_all | solution.py:83
  208.0 3.8 gather_fusion
  211.8 3.1 reshape.413
  216.3 3.9 multiply_reduce_fusion.5
  221.5 41.1 %all-reduce.16.cloned.1.call-done = f32[394,768]{1,0:T(8,128)} async-done(((f32[394,768]{1,0:T(8,128)}), f32[394,768]{1,0:T(8,128)}) %all-reduce.16.cloned.1.call-update) | async-done | bytes 1210384 | tf_op jit(solution)/shard_map/psum | solution.py:86
  279.7 8.1 gather_fusion.7
  288.3 33.4 %all-reduce.18.cloned.1.call-done = f32[394,768]{1,0:T(8,128)} async-done(((f32[394,768]{1,0:T(8,128)}), f32[394,768]{1,0:T(8,128)}) %all-reduce.18.cloned.1.call-update) | async-done | bytes 1210384 | tf_op jit(solution)/shard_map/psum | solution.py:59
  326.6 7.5 scatter_custom_fusion.1
  334.1 5.8 all-to-all-start.2
  342.0 4.1 mul.501
  346.4 8.1 gather_fusion.6
  355.0 10.8 scatter_custom_fusion.2
  365.7 11.1 all-to-all-done.2
  376.9 4.5 all-to-all-start.4
  381.4 7.5 multiply_convert_fusion
  388.9 29.1 %all-to-all-done.4 = bf16[8,128,768]{2,1,0:T(8,128)(2,1)} async-done(((bf16[8,128,768]{2,1,0:T(8,128)(2,1)}), bf16[8,128,768]{2,1,0:T(8,128)(2,1)}, u32[]{:S(2)}, u32[]{:S(2)}) %all-to-all-start.4) | async-done | bytes 1572896 | tf_op jit(solution)/shard_map/all_to_all | solution.py:136
  418.0 8.5 fusion.13
  428.2 4.3 fusion.16
  432.5 3.7 all-to-all-start.5
  436.1 6.9 fusion.18
  443.0 64.0 %all-to-all-done.5 = f32[8,128,768]{2,1,0:T(8,128)S(1)} async-done(((f32[8,128,768]{2,1,0:T(8,128)}), f32[8,128,768]{2,1,0:T(8,128)S(1)}, u32[]{:S(2)}, u32[]{:S(2)}) %all-to-all-start.5) | async-done | bytes 3145760 | tf_op jit(solution)/shard_map/all_to_all | solution.py:157
  508.7 3.6 all-to-all-start.3
  512.4 6.9 gather_fusion.2
  519.2 4.0 reshape.425
  523.2 5.6 reduce_sum.406
  531.1 52.1 %all-to-all-done.3 = f32[8,128,768]{2,1,0:T(8,128)S(1)} async-done(((f32[8,128,768]{2,1,0:T(8,128)}), f32[8,128,768]{2,1,0:T(8,128)S(1)}, u32[]{:S(2)}, u32[]{:S(2)}) %all-to-all-start.3) | async-done | bytes 3145760 | tf_op jit(solution)/shard_map/all_to_all | solution.py:83
  583.2 3.8 gather_fusion.1
  587.0 4.1 reshape.421
  591.1 8.1 multiply_reduce_fusion.3
  599.2 9.9 psum.103
  625.0 3.5 fusion.71
  629.0 42.9 %all-reduce.22.cloned.1.call-done = f32[394,768]{1,0:T(8,128)} async-done(((f32[394,768]{1,0:T(8,128)}), f32[394,768]{1,0:T(8,128)}) %all-reduce.22.cloned.1.call-update) | async-done | bytes 1210384 | tf_op jit(solution)/shard_map/psum | solution.py:231
  678.7 3.2 mul.539
  681.9 8.9 scatter_custom_fusion.3
  690.8 42.5 %all_to_all.41 = bf16[8,128,768]{2,1,0:T(8,128)(2,1)S(1)} all-to-all(bf16[8,128,768]{2,1,0:T(8,128)(2,1)} %bitcast.270), channel_id=1, replica_groups=mesh['tensor'=2,'expert'=8,'replica'=2] {'expert'}, dimensions={0} | all-to-all | bytes 3145728 | tf_op jit(solution)/shard_map/all_to_all | solution.py:136
  733.3 9.1 fusion.6
  745.1 74.1 %all_to_all.42 = f32[8,128,768]{2,1,0:T(8,128)S(1)} all-to-all(f32[8,128,768]{2,1,0:T(8,128)S(1)} %fusion.14), channel_id=1, replica_groups=mesh['tensor'=2,'expert'=8,'replica'=2] {'expert'}, dimensions={0} | all-to-all | bytes 6291456 | tf_op jit(solution)/shard_map/all_to_all | solution.py:157
  819.2 3.8 gather_fusion.3
  823.0 4.0 reshape.430
  827.0 5.7 reduce_sum.415
  832.9 3.1 multiply_reduce_fusion.2
  836.0 14.5 %psum.106 = f32[394,2]{1,0:T(8,128)S(1)} all-reduce(f32[394,2]{1,0:T(8,128)S(1)} %multiply_reduce_fusion.2), channel_id=1, replica_groups=mesh['tensor'=2,'expert'=8,'replica'=2] {'tensor'}, use_global_device_ids=true, to_apply=%region_47.50 | all-reduce | flops 788 | bytes 6304 | tf_op jit(solution)/shard_map/psum | solution.py:162
  850.8 27.6 %all-reduce.24.cloned.1.call-done = f32[394,768]{1,0:T(8,128)} async-done(((f32[394,768]{1,0:T(8,128)}), f32[394,768]{1,0:T(8,128)}) %all-reduce.24.cloned.1.call-update) | async-done | bytes 1210384 | tf_op jit(solution)/shard_map/psum | solution.py:162
  893.2 3.9 fusion.68
  905.3 3.4 pad_maximum_fusion.2
  908.9 5.2 convolution_bitcast_fusion
  916.9 4.2 pad_maximum_fusion.1
  921.4 5.2 convolution_bitcast_fusion.2
  929.3 4.5 pad_maximum_fusion
  935.3 32.9 %all-reduce.28.cloned.1.call-done = (f32[394,768]{1,0:T(8,128)}, f32[394,768]{1,0:T(8,128)}) async-done(((f32[394,768]{1,0:T(8,128)}, f32[394,768]{1,0:T(8,128)}), (f32[394,768]{1,0:T(8,128)}, f32[394,768]{1,0:T(8,128)})) %all-reduce.28.cloned.1.call-update) | async-done | bytes 2420752 | tf_op jit(solution)/shard_map/psum | solution.py:86
  970.7 65.3 %all-reduce.2 = (f32[2,2,768]{2,1,0:T(2,128)}, f32[2,768,8]{1,2,0:T(8,128)}) all-reduce(f32[2,2,768]{2,1,0:T(2,128)S(1)} %pad_maximum_fusion.5, f32[2,768,8]{1,2,0:T(8,128)S(1)} %pad_maximum_fusion.4), channel_id=1, replica_groups=mesh['tensor'=2,'expert'=8,'replica'=2] {'expert','replica'}, use_global_device_ids=true, to_apply=%region_60.63 | all-reduce | flops 15360 | bytes 122880 | tf_op jit(solution)/shard_map/psum | solution.py:248
  1036.0 3.4 add_add_fusion.4
  1039.5 118.8 %all-reduce.26.cloned.1.call-done = (f32[2,3,768,384]{2,3,1,0:T(8,128)}, f32[2,384,768]{2,1,0:T(8,128)}) async-done(((f32[2,3,768,384]{2,3,1,0:T(8,128)}, f32[2,384,768]{2,1,0:T(8,128)}), (f32[2,3,768,384]{2,3,1,0:T(8,128)}, f32[2,384,768]{2,1,0:T(8,128)})) %all-reduce.26.cloned.1.call-update) | async-done | bytes 9437200 | tf_op jit(solution)/shard_map/psum | solution.py:248
  1158.3 8.2 copy.267
  1166.5 12.7 %reduce-scatter.5.cloned.1.call-done = f32[2,1536,384]{2,1,0:T(8,128)} async-done(((f32[2,1536,768]{2,1,0:T(8,128)}), f32[2,1536,384]{2,1,0:T(8,128)}) %reduce-scatter.5.cloned.1.call-update) | async-done | bytes 4718608 | tf_op jit(solution)/shard_map/reduce_scatter | solution.py:246
  1179.1 22.0 %reduce-scatter.3.cloned.1.call-done = f32[2,384,1536]{2,1,0:T(8,128)} async-done(((f32[2,768,1536]{2,1,0:T(8,128)}), f32[2,384,1536]{2,1,0:T(8,128)}) %reduce-scatter.3.cloned.1.call-update) | async-done | bytes 4718608 | tf_op jit(solution)/shard_map/reduce_scatter | solution.py:245
  (459 shorter events, 119.6 us)
Async XLA Ops:
  7.2 61.4 %all-reduce.14.cloned.1.call-start = ((), (), s32[]{:S(2)}) async-start(), calls=%async_computation.10 | async-start | bytes 2457600 | tf_op jit(solution)/shard_map/psum | solution.py:59
  8.5 5.6 copy-start.94
  11.3 59.1 %copy-start.85 = (f32[768]{0:T(1024)}, f32[768]{0:T(1024)S(1)}, u32[]{:S(2)}) copy-start(f32[768]{0:T(1024)S(1)} %get-tuple-element.61) | copy-start | bytes 9220
  24.5 44.1 %copy-start.14 = (bf16[394,768]{1,0:T(8,128)(2,1)S(1)}, bf16[394,768]{1,0:T(8,128)(2,1)}, u32[]{:S(2)}) copy-start(bf16[394,768]{1,0:T(8,128)(2,1)} %param.13) | copy-start | bytes 1815556
  33.1 104.6 %copy-start.116 = (s32[788]{0:T(1024)}, s32[788]{0:T(1024)S(1)}, u32[]{:S(2)}) copy-start(s32[788]{0:T(1024)S(1)} %fusion.150) | copy-start | bytes 9460
  79.4 50.2 %slice-start = ((s8[4718592]{0:T(1024)(128)(4,1)}), s8[4194304]{0:T(1024)(128)(4,1)S(1)}, s32[]{:S(2)}) async-start(s8[4718592]{0:T(1024)(128)(4,1)} %bitcast.280), calls=%async_computation.20 | async-start | bytes 8388608
  122.0 7.6 copy-start.32
  122.0 7.6 slice-start.1
  133.9 74.1 %all-to-all-start.1 = ((f32[8,128,768]{2,1,0:T(8,128)}), f32[8,128,768]{2,1,0:T(8,128)S(1)}, u32[]{:S(2)}, u32[]{:S(2)}) async-start(f32[8,128,768]{2,1,0:T(8,128)} %fusion.20), calls=%async_computation.1 | async-start | bytes 6291456 | tf_op jit(solution)/shard_map/all_to_all | solution.py:83
  137.7 124.9 %all-reduce.16.cloned.1.call-start = ((), (), s32[]{:S(2)}) async-start(), calls=%async_computation.11 | async-start | bytes 2457600 | tf_op jit(solution)/shard_map/psum | solution.py:86
  137.7 70.2 %copy-start.100 = (s32[1024]{0:T(1024)}, s32[1024]{0:T(1024)S(1)}, u32[]{:S(2)}) copy-start(s32[1024]{0:T(1024)S(1)} %pad_clamp_fusion.1) | copy-start | bytes 12292
  139.7 8.4 copy-start.106
  220.3 42.3 %copy-start.9 = (f32[394,768]{1,0:T(8,128)S(1)}, f32[394,768]{1,0:T(8,128)}, u32[]{:S(2)}) copy-start(f32[394,768]{1,0:T(8,128)} %copy-done.8) | copy-start | bytes 3631108
  220.3 101.4 %all-reduce.18.cloned.1.call-start = ((), (), s32[]{:S(2)}) async-start(), calls=%async_computation.12 | async-start | bytes 2457600 | tf_op jit(solution)/shard_map/psum | solution.py:59
  221.5 43.1 %copy-start.83 = (f32[768]{0:T(1024)S(1)}, f32[768]{0:T(1024)}, u32[]{:S(2)}) copy-start(f32[768]{0:T(1024)} %get-tuple-element.63) | copy-start | bytes 9220
  264.2 57.4 %copy-start.11 = (f32[394,768]{1,0:T(8,128)}, f32[394,768]{1,0:T(8,128)S(1)}, u32[]{:S(2)}) copy-start(f32[394,768]{1,0:T(8,128)S(1)} %get-tuple-element.79) | copy-start | bytes 3631108
  267.0 5.7 copy-start.45
  288.3 36.0 %copy-start.87 = (f32[768]{0:T(1024)S(1)}, f32[768]{0:T(1024)}, u32[]{:S(2)}) copy-start(f32[768]{0:T(1024)} %get-tuple-element.60) | copy-start | bytes 9220
  324.4 21.6 %copy-start.30 = (bf16[394,768]{1,0:T(8,128)(2,1)}, bf16[394,768]{1,0:T(8,128)(2,1)S(1)}, u32[]{:S(2)}) copy-start(bf16[394,768]{1,0:T(8,128)(2,1)S(1)} %multiply_convert_fusion.6) | copy-start | bytes 1815556
  334.1 5.9 copy-start.24
  334.1 42.8 %all-to-all-start.2 = ((bf16[8,128,768]{2,1,0:T(8,128)(2,1)}), bf16[8,128,768]{2,1,0:T(8,128)(2,1)S(1)}, u32[]{:S(2)}, u32[]{:S(2)}) async-start(bf16[8,128,768]{2,1,0:T(8,128)(2,1)} %bitcast.268), calls=%async_computation.2 | async-start | bytes 3145728 | tf_op jit(solution)/shard_map/all_to_all | solution.py:74
  376.9 12.0 copy-start.34
  376.9 41.2 %all-to-all-start.4 = ((bf16[8,128,768]{2,1,0:T(8,128)(2,1)}), bf16[8,128,768]{2,1,0:T(8,128)(2,1)}, u32[]{:S(2)}, u32[]{:S(2)}) async-start(bf16[8,128,768]{2,1,0:T(8,128)(2,1)} %bitcast.269), calls=%async_computation.4 | async-start | bytes 3145728 | tf_op jit(solution)/shard_map/all_to_all | solution.py:136
  381.4 46.8 %slice-start.2 = ((s8[4718592]{0:T(1024)(128)(4,1)}), s8[524288]{0:T(1024)(128)(4,1)S(1)}, s32[]{:S(2)}) async-start(s8[4718592]{0:T(1024)(128)(4,1)} %bitcast.282), calls=%async_computation.22 | async-start | bytes 1048576
  418.0 10.1 slice-start.3
  432.5 74.5 %all-to-all-start.5 = ((f32[8,128,768]{2,1,0:T(8,128)}), f32[8,128,768]{2,1,0:T(8,128)S(1)}, u32[]{:S(2)}, u32[]{:S(2)}) async-start(f32[8,128,768]{2,1,0:T(8,128)} %fusion.16), calls=%async_computation.5 | async-start | bytes 6291456 | tf_op jit(solution)/shard_map/all_to_all | solution.py:157
  508.7 74.5 %all-to-all-start.3 = ((f32[8,128,768]{2,1,0:T(8,128)}), f32[8,128,768]{2,1,0:T(8,128)S(1)}, u32[]{:S(2)}, u32[]{:S(2)}) async-start(f32[8,128,768]{2,1,0:T(8,128)} %fusion.18), calls=%async_computation.3 | async-start | bytes 6291456 | tf_op jit(solution)/shard_map/all_to_all | solution.py:83
  512.3 97.0 %all-reduce.20.cloned.1.call-start = ((), (), s32[]{:S(2)}) async-start(), calls=%async_computation.13 | async-start | bytes 2457600 | tf_op jit(solution)/shard_map/psum | solution.py:162
  528.9 143.0 %all-reduce.22.cloned.1.call-start = ((), (), s32[]{:S(2)}) async-start(), calls=%async_computation.14 | async-start | bytes 2457600 | tf_op jit(solution)/shard_map/psum | solution.py:231
  591.1 18.1 %copy-start.99 = (s32[394,2]{0,1:T(2,128)S(1)}, s32[394,2]{0,1:T(2,128)}, u32[]{:S(2)}) copy-start(s32[394,2]{0,1:T(2,128)} %copy-done.98) | copy-start | bytes 9460
  591.1 18.2 %copy-start.6 = (f32[394,768]{1,0:T(8,128)S(1)}, f32[394,768]{1,0:T(8,128)}, u32[]{:S(2)}) copy-start(f32[394,768]{1,0:T(8,128)} %copy-done.5) | copy-start | bytes 3631108
  625.0 46.9 %copy-start.84 = (f32[768]{0:T(1024)S(1)}, f32[768]{0:T(1024)}, u32[]{:S(2)}) copy-start(f32[768]{0:T(1024)} %get-tuple-element.63) | copy-start | bytes 9220
  625.0 46.9 %copy-start.89 = (f32[394]{0:T(512)S(1)}, f32[394]{0:T(512)}, u32[]{:S(2)}) copy-start(f32[394]{0:T(512)} %copy-done.88) | copy-start | bytes 4732
  625.0 46.9 %copy-start.103 = (f32[394]{0:T(512)S(1)}, f32[394]{0:T(512)}, u32[]{:S(2)}) copy-start(f32[394]{0:T(512)} %copy-done.102) | copy-start | bytes 4732
  628.6 43.3 %copy-start.12 = (f32[394,768]{1,0:T(8,128)S(1)}, f32[394,768]{1,0:T(8,128)}, u32[]{:S(2)}) copy-start(f32[394,768]{1,0:T(8,128)} %copy-done.11) | copy-start | bytes 3631108
  628.6 45.2 %copy-start.113 = (f32[394]{0:T(512)S(1)}, f32[394]{0:T(512)}, u32[]{:S(2)}) copy-start(f32[394]{0:T(512)} %copy-done.112) | copy-start | bytes 4732
  628.6 249.8 %all-reduce.24.cloned.1.call-start = ((), (), s32[]{:S(2)}) async-start(), calls=%async_computation.15 | async-start | bytes 2457600 | tf_op jit(solution)/shard_map/psum | solution.py:162
  681.9 60.6 %slice-start.4 = ((s8[4718592]{0:T(1024)(128)(4,1)}), s8[524288]{0:T(1024)(128)(4,1)S(1)}, s32[]{:S(2)}) async-start(s8[4718592]{0:T(1024)(128)(4,1)} %bitcast.284), calls=%async_computation.24 | async-start | bytes 1048576
  733.3 9.1 copy-start.61
  733.3 9.1 slice-start.5
  745.1 74.1 %copy-start.101 = (s32[1024]{0:T(1024)S(1)}, s32[1024]{0:T(1024)}, u32[]{:S(2)}) copy-start(s32[1024]{0:T(1024)} %copy-done.100) | copy-start | bytes 12292
  827.0 5.8 copy-start.71
  827.0 5.8 copy-start.80
  827.0 5.8 copy-start.18
  832.7 135.4 %all-reduce.28.cloned.1.call-start = ((), (), s32[]{:S(2)}) async-start(), calls=%async_computation.19 | async-start | bytes 4915200 | tf_op jit(solution)/shard_map/psum | solution.py:86
  832.8 17.8 %copy-start.97 = (s32[394,2]{0,1:T(2,128)S(1)}, s32[394,2]{0,1:T(2,128)}, u32[]{:S(2)}) copy-start(s32[394,2]{0,1:T(2,128)} %copy-done.96) | copy-start | bytes 9460
  832.9 17.8 %copy-start.69 = (f32[394,8]{0,1:T(8,128)S(1)}, f32[394,8]{0,1:T(8,128)}, u32[]{:S(2)}) copy-start(f32[394,8]{0,1:T(8,128)} %copy-done.68) | copy-start | bytes 37828
  832.9 17.8 %copy-start.93 = (f32[394]{0:T(512)S(1)}, f32[394]{0:T(512)}, u32[]{:S(2)}) copy-start(f32[394]{0:T(512)} %copy-done.92) | copy-start | bytes 4732
  832.9 17.8 %copy-start.107 = (f32[394]{0:T(512)S(1)}, f32[394]{0:T(512)}, u32[]{:S(2)}) copy-start(f32[394]{0:T(512)} %copy-done.106) | copy-start | bytes 4732
  832.9 45.5 %copy-start.10 = (f32[394,768]{1,0:T(8,128)S(1)}, f32[394,768]{1,0:T(8,128)}, u32[]{:S(2)}) copy-start(f32[394,768]{1,0:T(8,128)} %copy-done.8) | copy-start | bytes 3631108
  832.9 45.5 %copy-start.86 = (f32[768]{0:T(1024)S(1)}, f32[768]{0:T(1024)}, u32[]{:S(2)}) copy-start(f32[768]{0:T(1024)} %copy-done.85) | copy-start | bytes 9220
  832.9 45.5 %copy-start.91 = (f32[394]{0:T(512)S(1)}, f32[394]{0:T(512)}, u32[]{:S(2)}) copy-start(f32[394]{0:T(512)} %copy-done.90) | copy-start | bytes 4732
  832.9 45.5 %copy-start.105 = (f32[394]{0:T(512)S(1)}, f32[394]{0:T(512)}, u32[]{:S(2)}) copy-start(f32[394]{0:T(512)} %copy-done.104) | copy-start | bytes 4732
  850.8 29.5 %copy-start.111 = (f32[394]{0:T(512)S(1)}, f32[394]{0:T(512)}, u32[]{:S(2)}) copy-start(f32[394]{0:T(512)} %copy-done.110) | copy-start | bytes 4732
  897.1 261.2 %all-reduce.26.cloned.1.call-start = ((), (), s32[]{:S(2)}) async-start(), calls=%async_computation.18 | async-start | bytes 18874368 | tf_op jit(solution)/shard_map/psum | solution.py:248
  908.8 5.3 copy-start.62
  908.8 270.3 %reduce-scatter.5.cloned.1.call-start = ((), (), s32[]{:S(2)}) async-start(), calls=%async_computation.17 | async-start | bytes 14155776 | tf_op jit(solution)/shard_map/reduce_scatter | solution.py:246
  908.8 5.3 copy-start.120
  921.2 5.5 copy-start.33
  921.2 280.0 %reduce-scatter.3.cloned.1.call-start = ((), (), s32[]{:S(2)}) async-start(), calls=%async_computation.16 | async-start | bytes 14155776 | tf_op jit(solution)/shard_map/reduce_scatter | solution.py:245
  921.4 5.2 copy-start.55
  934.9 35.1 %copy-start.109 = (f32[394]{0:T(512)S(1)}, f32[394]{0:T(512)}, u32[]{:S(2)}) copy-start(f32[394]{0:T(512)} %copy-done.108) | copy-start | bytes 4732
  968.2 67.8 %copy-start.7 = (f32[394,768]{1,0:T(8,128)S(1)}, f32[394,768]{1,0:T(8,128)}, u32[]{:S(2)}) copy-start(f32[394,768]{1,0:T(8,128)} %copy-done.5) | copy-start | bytes 3631108
  1158.3 42.9 %copy-start.56 = (f32[2,384,768]{2,1,0:T(8,128)S(1)}, f32[2,384,768]{2,1,0:T(8,128)}, u32[]{:S(2)}) copy-start(f32[2,384,768]{2,1,0:T(8,128)} %get-tuple-element.116) | copy-start | bytes 7077892
  (78 other events, 137.3 us)
Sparse Core Ops, SparseCore 0:
  21.9 46.6 all-reduce.13
  220.4 42.0 all-reduce.15
  277.6 43.9 all-reduce.17
  529.0 44.3 all-reduce.19
  628.7 43.1 all-reduce.21
  832.9 45.4 all-reduce.23
  897.2 70.9 all-reduce.27
  972.5 185.7 all-reduce.25
  1161.2 17.8 reduce-scatter.4
  1181.9 19.1 reduce-scatter.2
where the time goes:
time: 1220 us; the launch traced here: 1210 us
  waiting for transfers between devices  581 us (48%)
  blocking collectives  249 us (20%)
  local copies, waits for them, and re-layouts  154 us (13%)
  matrix products  98.9 us (8%)
  other arithmetic  88.1 us (7%)
  starting transfers between devices  22.7 us (2%)
  between operations  16.4 us (1%)
    psum x1, waiting for transfers between devices, on_device(): lax.psum((stacked[2], stacked[3], stacked[4], stacked[5]), ('expert', 're...  119 us
    all_to_all x2, waiting for transfers between devices, on_device(): lax.all_to_all(expert_part, 'expert', split_axis=0, concat_axis=0, tiled=...  109 us
    all_to_all x1, blocking collectives, on_device(): lax.all_to_all(input_grad, 'expert', split_axis=0, concat_axis=0, tiled=T...  74.1 us
    psum x2, waiting for transfers between devices, on_device(): residual = residual + lax.psum(moe_part, 'tensor')  74 us
    psum x2, waiting for transfers between devices, on_device(): residual = residual + lax.psum(attn_part, 'tensor')  68.9 us
    psum x1, blocking collectives, on_device(): lax.psum((stacked[2], stacked[3], stacked[4], stacked[5]), ('expert', 're...  65.3 us
    all_to_all x1, waiting for transfers between devices, on_device(): lax.all_to_all(input_grad, 'expert', split_axis=0, concat_axis=0, tiled=T...  64 us
    psum x1, waiting for transfers between devices, on_device(): norm_grad = lax.psum(norm_grad, 'tensor')  42.9 us
  transfers between devices with their start and end apart: 15, of which 14 were waited for; matrix products, arithmetic and copies ran while one was open for 13% of the time, Pallas kernels for 0%

commit v1 on v0

--- a/solution.py
+++ b/solution.py
@@ -71,7 +71,20 @@
             .set(jnp.repeat(moe_bf, 2, axis=0))
             .reshape(expert_count, capacity, model_width)
         )
-        received = lax.all_to_all(send_buffer, "expert", split_axis=0, concat_axis=0, tiled=True)
+        ways, here = (lax.axis_size("expert"), lax.axis_index("expert"))
+        width = send_buffer.shape[0] // ways
+        shape = list(send_buffer.shape)
+        shape[0] = width
+        height = shape[0]
+        shape[0] = height * ways
+        received = jnp.zeros(shape, send_buffer.dtype)
+        for mask in range(ways):
+            part = lax.dynamic_slice_in_dim(send_buffer, (here ^ mask) * width, width, axis=0)
+            if mask:
+                part = lax.ppermute(part, "expert", [(d, d ^ mask) for d in range(ways)])
+            received = lax.dynamic_update_slice_in_dim(
+                received, part, (here ^ mask) * height, axis=0
+            )
         source_count = received.shape[0]
         flat_in = received.reshape(-1, model_width)
         pre_act = jnp.dot(flat_in, expert_in[layer_index, 0], preferred_element_type=jnp.float32)

time: 1220 us -> 1220 us (level)
  blocking collectives: 249 us -> 206 us
  waiting for transfers between devices: 581 us -> 607 us
  starting transfers between devices: 22.7 us -> 46.7 us
    ppermute x0 -> x14, waiting for transfers between devices: none -> 75.3 us  [on_device(): part = lax.ppermute(part, 'expert', [(d, d ^ mask) for d in range(ways)])]
    all_to_all x1 -> x0, blocking collectives: 42.6 us -> none  [on_device(): lax.all_to_all(send_buffer, 'expert', split_axis=0, concat_axis=0, tiled=...]
    all_to_all x1, waiting for transfers between devices: 29.1 us -> 0.01 us  [on_device(): lax.all_to_all(grad_send, 'expert', split_axis=0, concat_axis=0, tiled=True)]
    ppermute x0 -> x14, starting transfers between devices: none -> 27.7 us  [on_device(): part = lax.ppermute(part, 'expert', [(d, d ^ mask) for d in range(ways)])]
    unnamed x262 -> x300, local copies, waits for them, and re-layouts: 32.4 us -> 34.8 us
  transfers between devices with their start and end apart: 15 -> 28, of which waited for: 14 -> 18; matrix products, arithmetic and copies ran while one was open for 13% -> 12% of each run, Pallas kernels for 0% -> 0%
where the time goes in v1:
time: 1220 us
  waiting for transfers between devices  607 us (50%)
  blocking collectives  206 us (17%)
  local copies, waits for them, and re-layouts  152 us (12%)
  matrix products  99.2 us (8%)
  other arithmetic  88.1 us (7%)
  starting transfers between devices  46.7 us (4%)
  between operations  16.8 us (1%)
    psum x1, waiting for transfers between devices, on_device(): lax.psum((stacked[2], stacked[3], stacked[4], stacked[5]), ('expert', 're...  118 us
    all_to_all x2, waiting for transfers between devices, on_device(): lax.all_to_all(expert_part, 'expert', split_axis=0, concat_axis=0, tiled=...  109 us
    ppermute x14, waiting for transfers between devices, on_device(): part = lax.ppermute(part, 'expert', [(d, d ^ mask) for d in range(ways)])  75.3 us
    psum x2, waiting for transfers between devices, on_device(): residual = residual + lax.psum(moe_part, 'tensor')  74.2 us
    all_to_all x1, blocking collectives, on_device(): lax.all_to_all(input_grad, 'expert', split_axis=0, concat_axis=0, tiled=T...  74.1 us
    psum x1, blocking collectives, on_device(): lax.psum((stacked[2], stacked[3], stacked[4], stacked[5]), ('expert', 're...  65.3 us
    all_to_all x1, waiting for transfers between devices, on_device(): lax.all_to_all(input_grad, 'expert', split_axis=0, concat_axis=0, tiled=T...  64 us
    psum x2, waiting for transfers between devices, on_device(): residual = residual + lax.psum(attn_part, 'tensor')  60.9 us
  transfers between devices with their start and end apart: 28, of which 18 were waited for; matrix products, arithmetic and copies ran while one was open for 12% of the time, Pallas kernels for 0%

profile of v1, /device:TPU:0, one launch (start us, length us, event | category | flops | bytes accessed | tf_op | source)
XLA Modules:
  0.0 1215.7 jit_solution(1305284106616068543)
XLA Ops:
  27.1 8.1 gather_fusion.5
  36.0 8.1 gather_fusion.7
  45.2 23.4 %all-reduce.14.cloned.1.call-done = f32[394,768]{1,0:T(8,128)} async-done(((f32[394,768]{1,0:T(8,128)}), f32[394,768]{1,0:T(8,128)}) %all-reduce.14.cloned.1.call-update) | async-done | bytes 1210384 | tf_op jit(solution)/shard_map/psum | solution.py:59
  73.3 6.1 scatter_custom_fusion
  88.0 4.2 collective-permute-start.2
  92.3 13.6 %collective-permute-done.2 = bf16[1,128,768]{2,1,0:T(8,128)(2,1)S(1)} collective-permute-done((bf16[1,128,768]{2,1,0:T(8,128)(2,1)S(1)}, bf16[1,128,768]{2,1,0:T(8,128)(2,1)S(1)}, u32[]{:S(2)}, u32[]{:S(2)}) %collective-permute-start.2) | collective-permute-done | bytes 196640 | tf_op jit(solution)/shard_map/ppermute | solution.py:84
  105.9 13.7 %collective-permute-done.3 = bf16[1,128,768]{2,1,0:T(8,128)(2,1)S(1)} collective-permute-done((bf16[1,128,768]{2,1,0:T(8,128)(2,1)S(1)}, bf16[1,128,768]{2,1,0:T(8,128)(2,1)S(1)}, u32[]{:S(2)}, u32[]{:S(2)}) %collective-permute-start.3) | collective-permute-done | bytes 196640 | tf_op jit(solution)/shard_map/ppermute | solution.py:84
  119.8 7.7 multiply_convert_fusion.1
  127.5 4.3 fusion.20
  131.8 4.8 all-to-all-start
  138.6 8.1 gather_fusion.4
  149.3 56.8 %all-to-all-done = f32[8,128,768]{2,1,0:T(8,128)S(1)} async-done(((f32[8,128,768]{2,1,0:T(8,128)}), f32[8,128,768]{2,1,0:T(8,128)S(1)}, u32[]{:S(2)}, u32[]{:S(2)}) %all-to-all-start) | async-done | bytes 3145760 | tf_op jit(solution)/shard_map/all_to_all | solution.py:96
  206.2 3.8 gather_fusion
  214.5 4.0 multiply_reduce_fusion.5
  218.7 42.0 %all-reduce.16.cloned.1.call-done = f32[394,768]{1,0:T(8,128)} async-done(((f32[394,768]{1,0:T(8,128)}), f32[394,768]{1,0:T(8,128)}) %all-reduce.16.cloned.1.call-update) | async-done | bytes 1210384 | tf_op jit(solution)/shard_map/psum | solution.py:99
  274.2 4.5 mul.501
  278.7 37.6 %all-reduce.18.cloned.1.call-done = f32[394,768]{1,0:T(8,128)} async-done(((f32[394,768]{1,0:T(8,128)}), f32[394,768]{1,0:T(8,128)}) %all-reduce.18.cloned.1.call-update) | async-done | bytes 1210384 | tf_op jit(solution)/shard_map/psum | solution.py:59
  319.5 8.1 gather_fusion.6
  329.6 8.8 scatter_custom_fusion.2
  338.4 5.5 all-to-all-start.2
  345.0 6.3 scatter_custom_fusion.1
  364.6 10.9 collective-permute-done.8
  375.5 4.2 collective-permute-start.10
  379.7 14.1 %collective-permute-done.9 = bf16[1,128,768]{2,1,0:T(8,128)(2,1)S(1)} collective-permute-done((bf16[1,128,768]{2,1,0:T(8,128)(2,1)S(1)}, bf16[1,128,768]{2,1,0:T(8,128)(2,1)S(1)}, u32[]{:S(2)}, u32[]{:S(2)}) %collective-permute-start.9) | collective-permute-done | bytes 196640 | tf_op jit(solution)/shard_map/ppermute | solution.py:84
  393.8 20.8 %collective-permute-done.10 = bf16[1,128,768]{2,1,0:T(8,128)(2,1)S(1)} collective-permute-done((bf16[1,128,768]{2,1,0:T(8,128)(2,1)S(1)}, bf16[1,128,768]{2,1,0:T(8,128)(2,1)S(1)}, u32[]{:S(2)}, u32[]{:S(2)}) %collective-permute-start.10) | collective-permute-done | bytes 196640 | tf_op jit(solution)/shard_map/ppermute | solution.py:84
  415.9 7.5 multiply_convert_fusion
  423.4 8.5 fusion.13
  433.6 4.3 fusion.16
  437.9 3.7 all-to-all-start.3
  441.5 6.9 fusion.18
  448.4 64.0 %all-to-all-done.3 = f32[8,128,768]{2,1,0:T(8,128)S(1)} async-done(((f32[8,128,768]{2,1,0:T(8,128)}), f32[8,128,768]{2,1,0:T(8,128)S(1)}, u32[]{:S(2)}, u32[]{:S(2)}) %all-to-all-start.3) | async-done | bytes 3145760 | tf_op jit(solution)/shard_map/all_to_all | solution.py:170
  514.1 3.7 all-to-all-start.1
  518.0 6.6 gather_fusion.2
  524.6 4.0 reshape.425
  528.6 5.6 reduce_sum.406
  536.5 52.1 %all-to-all-done.1 = f32[8,128,768]{2,1,0:T(8,128)S(1)} async-done(((f32[8,128,768]{2,1,0:T(8,128)}), f32[8,128,768]{2,1,0:T(8,128)S(1)}, u32[]{:S(2)}, u32[]{:S(2)}) %all-to-all-start.1) | async-done | bytes 3145760 | tf_op jit(solution)/shard_map/all_to_all | solution.py:96
  588.6 3.8 gather_fusion.1
  592.4 4.1 reshape.421
  596.6 8.1 multiply_reduce_fusion.3
  604.7 9.8 psum.103
  631.1 3.6 fusion.71
  635.1 42.9 %all-reduce.22.cloned.1.call-done = f32[394,768]{1,0:T(8,128)} async-done(((f32[394,768]{1,0:T(8,128)}), f32[394,768]{1,0:T(8,128)}) %all-reduce.22.cloned.1.call-update) | async-done | bytes 1210384 | tf_op jit(solution)/shard_map/psum | solution.py:244
  684.9 3.2 mul.539
  688.0 8.9 scatter_custom_fusion.3
  696.9 42.5 %all_to_all.30 = bf16[8,128,768]{2,1,0:T(8,128)(2,1)S(1)} all-to-all(bf16[8,128,768]{2,1,0:T(8,128)(2,1)} %bitcast.271), channel_id=1, replica_groups=mesh['tensor'=2,'expert'=8,'replica'=2] {'expert'}, dimensions={0} | all-to-all | bytes 3145728 | tf_op jit(solution)/shard_map/all_to_all | solution.py:149
  739.5 9.1 fusion.6
  751.3 74.1 %all_to_all.31 = f32[8,128,768]{2,1,0:T(8,128)S(1)} all-to-all(f32[8,128,768]{2,1,0:T(8,128)S(1)} %fusion.14), channel_id=1, replica_groups=mesh['tensor'=2,'expert'=8,'replica'=2] {'expert'}, dimensions={0} | all-to-all | bytes 6291456 | tf_op jit(solution)/shard_map/all_to_all | solution.py:170
  825.3 3.8 gather_fusion.3
  829.1 4.0 reshape.430
  833.1 5.7 reduce_sum.415
  842.1 14.5 %psum.106 = f32[394,2]{1,0:T(8,128)S(1)} all-reduce(f32[394,2]{1,0:T(8,128)S(1)} %multiply_reduce_fusion.2), channel_id=1, replica_groups=mesh['tensor'=2,'expert'=8,'replica'=2] {'tensor'}, use_global_device_ids=true, to_apply=%region_47.50 | all-reduce | flops 788 | bytes 6304 | tf_op jit(solution)/shard_map/psum | solution.py:175
  856.9 27.6 %all-reduce.24.cloned.1.call-done = f32[394,768]{1,0:T(8,128)} async-done(((f32[394,768]{1,0:T(8,128)}), f32[394,768]{1,0:T(8,128)}) %all-reduce.24.cloned.1.call-update) | async-done | bytes 1210384 | tf_op jit(solution)/shard_map/psum | solution.py:175
  899.3 3.9 fusion.68
  911.4 3.4 pad_maximum_fusion.2
  914.9 5.2 convolution_bitcast_fusion
  923.0 4.3 pad_maximum_fusion.1
  928.7 4.7 convolution_bitcast_fusion.2
  936.1 4.5 pad_maximum_fusion
  942.1 32.2 %all-reduce.28.cloned.1.call-done = (f32[394,768]{1,0:T(8,128)}, f32[394,768]{1,0:T(8,128)}) async-done(((f32[394,768]{1,0:T(8,128)}, f32[394,768]{1,0:T(8,128)}), (f32[394,768]{1,0:T(8,128)}, f32[394,768]{1,0:T(8,128)})) %all-reduce.28.cloned.1.call-update) | async-done | bytes 2420752 | tf_op jit(solution)/shard_map/psum | solution.py:99
  976.8 65.3 %all-reduce.2 = (f32[2,2,768]{2,1,0:T(2,128)}, f32[2,768,8]{1,2,0:T(8,128)}) all-reduce(f32[2,2,768]{2,1,0:T(2,128)S(1)} %pad_maximum_fusion.5, f32[2,768,8]{1,2,0:T(8,128)S(1)} %pad_maximum_fusion.4), channel_id=1, replica_groups=mesh['tensor'=2,'expert'=8,'replica'=2] {'expert','replica'}, use_global_device_ids=true, to_apply=%region_60.63 | all-reduce | flops 15360 | bytes 122880 | tf_op jit(solution)/shard_map/psum | solution.py:261
  1046.0 118.4 %all-reduce.26.cloned.1.call-done = (f32[2,3,768,384]{2,3,1,0:T(8,128)}, f32[2,384,768]{2,1,0:T(8,128)}) async-done(((f32[2,3,768,384]{2,3,1,0:T(8,128)}, f32[2,384,768]{2,1,0:T(8,128)}), (f32[2,3,768,384]{2,3,1,0:T(8,128)}, f32[2,384,768]{2,1,0:T(8,128)})) %all-reduce.26.cloned.1.call-update) | async-done | bytes 9437200 | tf_op jit(solution)/shard_map/psum | solution.py:261
  1164.3 8.2 copy.267
  1172.5 12.7 %reduce-scatter.5.cloned.1.call-done = f32[2,1536,384]{2,1,0:T(8,128)} async-done(((f32[2,1536,768]{2,1,0:T(8,128)}), f32[2,1536,384]{2,1,0:T(8,128)}) %reduce-scatter.5.cloned.1.call-update) | async-done | bytes 4718608 | tf_op jit(solution)/shard_map/reduce_scatter | solution.py:259
  1185.2 22.0 %reduce-scatter.3.cloned.1.call-done = f32[2,384,1536]{2,1,0:T(8,128)} async-done(((f32[2,768,1536]{2,1,0:T(8,128)}), f32[2,384,1536]{2,1,0:T(8,128)}) %reduce-scatter.3.cloned.1.call-update) | async-done | bytes 4718608 | tf_op jit(solution)/shard_map/reduce_scatter | solution.py:258
  (541 shorter events, 152.4 us)
Async XLA Ops:
  7.2 61.4 %all-reduce.14.cloned.1.call-start = ((), (), s32[]{:S(2)}) async-start(), calls=%async_computation.8 | async-start | bytes 2457600 | tf_op jit(solution)/shard_map/psum | solution.py:59
  11.3 59.1 %copy-start.88 = (f32[768]{0:T(1024)}, f32[768]{0:T(1024)S(1)}, u32[]{:S(2)}) copy-start(f32[768]{0:T(1024)S(1)} %get-tuple-element.61) | copy-start | bytes 9220
  21.9 22.3 %copy-start.38 = (s32[1,394,2]{2,1,0:T(8,128)}, s32[1,394,2]{2,1,0:T(8,128)S(1)}, u32[]{:S(2)}) copy-start(s32[1,394,2]{2,1,0:T(8,128)S(1)} %copy.307) | copy-start | bytes 9460
  36.0 32.6 %copy-start.14 = (bf16[394,768]{1,0:T(8,128)(2,1)S(1)}, bf16[394,768]{1,0:T(8,128)(2,1)}, u32[]{:S(2)}) copy-start(bf16[394,768]{1,0:T(8,128)(2,1)} %param.13) | copy-start | bytes 1815556
  45.2 91.4 %copy-start.134 = (s32[788]{0:T(1024)}, s32[788]{0:T(1024)S(1)}, u32[]{:S(2)}) copy-start(s32[788]{0:T(1024)S(1)} %get-tuple-element.124) | copy-start | bytes 9460
  79.5 48.0 %slice-start = ((s8[4718592]{0:T(1024)(128)(4,1)}), s8[4194304]{0:T(1024)(128)(4,1)S(1)}, s32[]{:S(2)}) async-start(s8[4718592]{0:T(1024)(128)(4,1)} %bitcast.280), calls=%async_computation.18 | async-start | bytes 8388608
  79.6 8.4 collective-permute-start
  81.2 11.0 collective-permute-start.1
  82.6 37.1 %collective-permute-start.6 = (bf16[1,128,768]{2,1,0:T(8,128)(2,1)S(1)}, bf16[1,128,768]{2,1,0:T(8,128)(2,1)S(1)}, u32[]{:S(2)}, u32[]{:S(2)}) collective-permute-start(bf16[1,128,768]{2,1,0:T(8,128)(2,1)S(1)} %get-tuple-element.90), channel_id=1, source_target_pairs={{0,14},{2,12},{4,10},{6,8},{8,6},{10,4},{12,2},{14,0},{1,15},{3,13... | collective-permute-start | bytes 589832 | tf_op jit(solution)/shard_map/ppermute | solution.py:84
  85.0 34.7 %collective-permute-start.5 = (bf16[1,128,768]{2,1,0:T(8,128)(2,1)S(1)}, bf16[1,128,768]{2,1,0:T(8,128)(2,1)S(1)}, u32[]{:S(2)}, u32[]{:S(2)}) collective-permute-start(bf16[1,128,768]{2,1,0:T(8,128)(2,1)S(1)} %get-tuple-element.91), channel_id=1, source_target_pairs={{0,12},{2,14},{4,8},{6,10},{8,4},{10,6},{12,0},{14,2},{1,13},{3,15... | collective-permute-start | bytes 589832 | tf_op jit(solution)/shard_map/ppermute | solution.py:84
  86.5 33.2 %collective-permute-start.4 = (bf16[1,128,768]{2,1,0:T(8,128)(2,1)S(1)}, bf16[1,128,768]{2,1,0:T(8,128)(2,1)S(1)}, u32[]{:S(2)}, u32[]{:S(2)}) collective-permute-start(bf16[1,128,768]{2,1,0:T(8,128)(2,1)S(1)} %get-tuple-element.92), channel_id=1, source_target_pairs={{0,10},{2,8},{4,14},{6,12},{8,2},{10,0},{12,6},{14,4},{1,11},{3,9}... | collective-permute-start | bytes 589832 | tf_op jit(solution)/shard_map/ppermute | solution.py:84
  88.0 17.9 %collective-permute-start.2 = (bf16[1,128,768]{2,1,0:T(8,128)(2,1)S(1)}, bf16[1,128,768]{2,1,0:T(8,128)(2,1)S(1)}, u32[]{:S(2)}, u32[]{:S(2)}) collective-permute-start(bf16[1,128,768]{2,1,0:T(8,128)(2,1)S(1)} %get-tuple-element.94), channel_id=1, source_target_pairs={{0,6},{2,4},{4,2},{6,0},{8,14},{10,12},{12,10},{14,8},{1,7},{3,5},... | collective-permute-start | bytes 589832 | tf_op jit(solution)/shard_map/ppermute | solution.py:84
  92.2 27.4 %collective-permute-start.3 = (bf16[1,128,768]{2,1,0:T(8,128)(2,1)S(1)}, bf16[1,128,768]{2,1,0:T(8,128)(2,1)S(1)}, u32[]{:S(2)}, u32[]{:S(2)}) collective-permute-start(bf16[1,128,768]{2,1,0:T(8,128)(2,1)S(1)} %get-tuple-element.93), channel_id=1, source_target_pairs={{0,8},{2,10},{4,12},{6,14},{8,0},{10,2},{12,4},{14,6},{1,9},{3,11}... | collective-permute-start | bytes 589832 | tf_op jit(solution)/shard_map/ppermute | solution.py:84
  131.8 74.4 %all-to-all-start = ((f32[8,128,768]{2,1,0:T(8,128)}), f32[8,128,768]{2,1,0:T(8,128)S(1)}, u32[]{:S(2)}, u32[]{:S(2)}) async-start(f32[8,128,768]{2,1,0:T(8,128)} %fusion.20), calls=%async_computation | async-start | bytes 6291456 | tf_op jit(solution)/shard_map/all_to_all | solution.py:96
  136.5 124.2 %all-reduce.16.cloned.1.call-start = ((), (), s32[]{:S(2)}) async-start(), calls=%async_computation.9 | async-start | bytes 2457600 | tf_op jit(solution)/shard_map/psum | solution.py:99
  136.6 69.5 %copy-start.108 = (s32[1024]{0:T(1024)}, s32[1024]{0:T(1024)S(1)}, u32[]{:S(2)}) copy-start(s32[1024]{0:T(1024)S(1)} %pad_clamp_fusion.1) | copy-start | bytes 12292
  218.4 42.3 %copy-start.6 = (f32[394,768]{1,0:T(8,128)S(1)}, f32[394,768]{1,0:T(8,128)}, u32[]{:S(2)}) copy-start(f32[394,768]{1,0:T(8,128)} %copy-done.5) | copy-start | bytes 3631108
  218.5 45.0 %copy-start.86 = (f32[768]{0:T(1024)S(1)}, f32[768]{0:T(1024)}, u32[]{:S(2)}) copy-start(f32[768]{0:T(1024)} %get-tuple-element.63) | copy-start | bytes 9220
  218.5 97.8 %all-reduce.18.cloned.1.call-start = ((), (), s32[]{:S(2)}) async-start(), calls=%async_computation.10 | async-start | bytes 2457600 | tf_op jit(solution)/shard_map/psum | solution.py:59
  262.4 53.9 %copy-start.11 = (f32[394,768]{1,0:T(8,128)}, f32[394,768]{1,0:T(8,128)S(1)}, u32[]{:S(2)}) copy-start(f32[394,768]{1,0:T(8,128)S(1)} %get-tuple-element.79) | copy-start | bytes 3631108
  278.7 39.5 %copy-start.90 = (f32[768]{0:T(1024)S(1)}, f32[768]{0:T(1024)}, u32[]{:S(2)}) copy-start(f32[768]{0:T(1024)} %get-tuple-element.60) | copy-start | bytes 9220
  318.4 25.5 %copy-start.31 = (bf16[394,768]{1,0:T(8,128)(2,1)}, bf16[394,768]{1,0:T(8,128)(2,1)S(1)}, u32[]{:S(2)}) copy-start(bf16[394,768]{1,0:T(8,128)(2,1)S(1)} %multiply_convert_fusion.6) | copy-start | bytes 1815556
  338.4 85.0 %all-to-all-start.2 = ((bf16[8,128,768]{2,1,0:T(8,128)(2,1)}), bf16[8,128,768]{2,1,0:T(8,128)(2,1)}, u32[]{:S(2)}, u32[]{:S(2)}) async-start(bf16[8,128,768]{2,1,0:T(8,128)(2,1)} %bitcast.264), calls=%async_computation.2 | async-start | bytes 3145728 | tf_op jit(solution)/shard_map/all_to_all | solution.py:149
  351.5 11.0 collective-permute-start.7
  353.6 21.9 %collective-permute-start.8 = (bf16[1,128,768]{2,1,0:T(8,128)(2,1)S(1)}, bf16[1,128,768]{2,1,0:T(8,128)(2,1)S(1)}, u32[]{:S(2)}, u32[]{:S(2)}) collective-permute-start(bf16[1,128,768]{2,1,0:T(8,128)(2,1)S(1)} %get-tuple-element.87), channel_id=1, source_target_pairs={{0,4},{2,6},{4,0},{6,2},{8,12},{10,14},{12,8},{14,10},{1,5},{3,7},... | collective-permute-start | bytes 589832 | tf_op jit(solution)/shard_map/ppermute | solution.py:84
  355.1 59.7 %collective-permute-start.13 = (bf16[1,128,768]{2,1,0:T(8,128)(2,1)S(1)}, bf16[1,128,768]{2,1,0:T(8,128)(2,1)S(1)}, u32[]{:S(2)}, u32[]{:S(2)}) collective-permute-start(bf16[1,128,768]{2,1,0:T(8,128)(2,1)S(1)} %get-tuple-element.82), channel_id=1, source_target_pairs={{0,14},{2,12},{4,10},{6,8},{8,6},{10,4},{12,2},{14,0},{1,15},{3,13... | collective-permute-start | bytes 589832 | tf_op jit(solution)/shard_map/ppermute | solution.py:84
  357.5 57.3 %collective-permute-start.12 = (bf16[1,128,768]{2,1,0:T(8,128)(2,1)S(1)}, bf16[1,128,768]{2,1,0:T(8,128)(2,1)S(1)}, u32[]{:S(2)}, u32[]{:S(2)}) collective-permute-start(bf16[1,128,768]{2,1,0:T(8,128)(2,1)S(1)} %get-tuple-element.83), channel_id=1, source_target_pairs={{0,12},{2,14},{4,8},{6,10},{8,4},{10,6},{12,0},{14,2},{1,13},{3,15... | collective-permute-start | bytes 589832 | tf_op jit(solution)/shard_map/ppermute | solution.py:84
  358.9 55.8 %collective-permute-start.11 = (bf16[1,128,768]{2,1,0:T(8,128)(2,1)S(1)}, bf16[1,128,768]{2,1,0:T(8,128)(2,1)S(1)}, u32[]{:S(2)}, u32[]{:S(2)}) collective-permute-start(bf16[1,128,768]{2,1,0:T(8,128)(2,1)S(1)} %get-tuple-element.84), channel_id=1, source_target_pairs={{0,10},{2,8},{4,14},{6,12},{8,2},{10,0},{12,6},{14,4},{1,11},{3,9}... | collective-permute-start | bytes 589832 | tf_op jit(solution)/shard_map/ppermute | solution.py:84
  362.5 31.2 %collective-permute-start.9 = (bf16[1,128,768]{2,1,0:T(8,128)(2,1)S(1)}, bf16[1,128,768]{2,1,0:T(8,128)(2,1)S(1)}, u32[]{:S(2)}, u32[]{:S(2)}) collective-permute-start(bf16[1,128,768]{2,1,0:T(8,128)(2,1)S(1)} %get-tuple-element.86), channel_id=1, source_target_pairs={{0,6},{2,4},{4,2},{6,0},{8,14},{10,12},{12,10},{14,8},{1,7},{3,5},... | collective-permute-start | bytes 589832 | tf_op jit(solution)/shard_map/ppermute | solution.py:84
  375.5 39.1 %collective-permute-start.10 = (bf16[1,128,768]{2,1,0:T(8,128)(2,1)S(1)}, bf16[1,128,768]{2,1,0:T(8,128)(2,1)S(1)}, u32[]{:S(2)}, u32[]{:S(2)}) collective-permute-start(bf16[1,128,768]{2,1,0:T(8,128)(2,1)S(1)} %get-tuple-element.85), channel_id=1, source_target_pairs={{0,8},{2,10},{4,12},{6,14},{8,0},{10,2},{12,4},{14,6},{1,9},{3,11}... | collective-permute-start | bytes 589832 | tf_op jit(solution)/shard_map/ppermute | solution.py:84
  437.9 74.6 %all-to-all-start.3 = ((f32[8,128,768]{2,1,0:T(8,128)}), f32[8,128,768]{2,1,0:T(8,128)S(1)}, u32[]{:S(2)}, u32[]{:S(2)}) async-start(f32[8,128,768]{2,1,0:T(8,128)} %fusion.16), calls=%async_computation.3 | async-start | bytes 6291456 | tf_op jit(solution)/shard_map/all_to_all | solution.py:170
  514.1 74.5 %all-to-all-start.1 = ((f32[8,128,768]{2,1,0:T(8,128)}), f32[8,128,768]{2,1,0:T(8,128)S(1)}, u32[]{:S(2)}, u32[]{:S(2)}) async-start(f32[8,128,768]{2,1,0:T(8,128)} %fusion.18), calls=%async_computation.1 | async-start | bytes 6291456 | tf_op jit(solution)/shard_map/all_to_all | solution.py:96
  517.7 97.0 %all-reduce.20.cloned.1.call-start = ((), (), s32[]{:S(2)}) async-start(), calls=%async_computation.11 | async-start | bytes 2457600 | tf_op jit(solution)/shard_map/psum | solution.py:175
  534.2 143.7 %all-reduce.22.cloned.1.call-start = ((), (), s32[]{:S(2)}) async-start(), calls=%async_computation.12 | async-start | bytes 2457600 | tf_op jit(solution)/shard_map/psum | solution.py:244
  596.5 18.1 %copy-start.107 = (s32[394,2]{0,1:T(2,128)S(1)}, s32[394,2]{0,1:T(2,128)}, u32[]{:S(2)}) copy-start(s32[394,2]{0,1:T(2,128)} %copy-done.106) | copy-start | bytes 9460
  596.5 18.1 %copy-start.103 = (f32[394]{0:T(512)S(1)}, f32[394]{0:T(512)}, u32[]{:S(2)}) copy-start(f32[394]{0:T(512)} %copy-done.102) | copy-start | bytes 4732
  596.5 18.1 %copy-start.122 = (f32[394]{0:T(512)S(1)}, f32[394]{0:T(512)}, u32[]{:S(2)}) copy-start(f32[394]{0:T(512)} %copy-done.121) | copy-start | bytes 4732
  596.5 18.2 %copy-start.9 = (f32[394,768]{1,0:T(8,128)S(1)}, f32[394,768]{1,0:T(8,128)}, u32[]{:S(2)}) copy-start(f32[394,768]{1,0:T(8,128)} %copy-done.8) | copy-start | bytes 3631108
  596.5 18.2 %copy-start.91 = (f32[768]{0:T(1024)S(1)}, f32[768]{0:T(1024)}, u32[]{:S(2)}) copy-start(f32[768]{0:T(1024)} %get-tuple-element.60) | copy-start | bytes 9220
  596.5 18.2 %copy-start.99 = (f32[394]{0:T(512)S(1)}, f32[394]{0:T(512)}, u32[]{:S(2)}) copy-start(f32[394]{0:T(512)} %copy-done.98) | copy-start | bytes 4732
  596.5 18.2 %copy-start.117 = (f32[394]{0:T(512)S(1)}, f32[394]{0:T(512)}, u32[]{:S(2)}) copy-start(f32[394]{0:T(512)} %copy-done.116) | copy-start | bytes 4732
  618.0 62.5 %copy-start.110 = (f32[394]{0:T(512)}, f32[394]{0:T(512)S(1)}, u32[]{:S(2)}) copy-start(f32[394]{0:T(512)S(1)} %negate_multiply_fusion.3) | copy-start | bytes 4732
  631.1 46.9 %copy-start.87 = (f32[768]{0:T(1024)S(1)}, f32[768]{0:T(1024)}, u32[]{:S(2)}) copy-start(f32[768]{0:T(1024)} %get-tuple-element.63) | copy-start | bytes 9220
  631.1 46.9 %copy-start.95 = (f32[394]{0:T(512)S(1)}, f32[394]{0:T(512)}, u32[]{:S(2)}) copy-start(f32[394]{0:T(512)} %copy-done.94) | copy-start | bytes 4732
  631.1 46.9 %copy-start.113 = (f32[394]{0:T(512)S(1)}, f32[394]{0:T(512)}, u32[]{:S(2)}) copy-start(f32[394]{0:T(512)} %copy-done.112) | copy-start | bytes 4732
  634.6 43.4 %copy-start.12 = (f32[394,768]{1,0:T(8,128)S(1)}, f32[394,768]{1,0:T(8,128)}, u32[]{:S(2)}) copy-start(f32[394,768]{1,0:T(8,128)} %copy-done.11) | copy-start | bytes 3631108
  634.7 45.2 %copy-start.130 = (f32[394]{0:T(512)S(1)}, f32[394]{0:T(512)}, u32[]{:S(2)}) copy-start(f32[394]{0:T(512)} %copy-done.129) | copy-start | bytes 4732
  634.7 249.8 %all-reduce.24.cloned.1.call-start = ((), (), s32[]{:S(2)}) async-start(), calls=%async_computation.13 | async-start | bytes 2457600 | tf_op jit(solution)/shard_map/psum | solution.py:175
  688.0 60.6 %slice-start.4 = ((s8[4718592]{0:T(1024)(128)(4,1)}), s8[524288]{0:T(1024)(128)(4,1)S(1)}, s32[]{:S(2)}) async-start(s8[4718592]{0:T(1024)(128)(4,1)} %bitcast.284), calls=%async_computation.22 | async-start | bytes 1048576
  751.3 74.1 %copy-start.109 = (s32[1024]{0:T(1024)S(1)}, s32[1024]{0:T(1024)}, u32[]{:S(2)}) copy-start(s32[1024]{0:T(1024)} %copy-done.108) | copy-start | bytes 12292
  838.8 135.4 %all-reduce.28.cloned.1.call-start = ((), (), s32[]{:S(2)}) async-start(), calls=%async_computation.17 | async-start | bytes 4915200 | tf_op jit(solution)/shard_map/psum | solution.py:99
  838.9 17.9 %copy-start.74 = (f32[394,8]{0,1:T(8,128)S(1)}, f32[394,8]{0,1:T(8,128)}, u32[]{:S(2)}) copy-start(f32[394,8]{0,1:T(8,128)} %copy-done.73) | copy-start | bytes 37828
  839.0 17.9 %copy-start.101 = (f32[394]{0:T(512)S(1)}, f32[394]{0:T(512)}, u32[]{:S(2)}) copy-start(f32[394]{0:T(512)} %copy-done.100) | copy-start | bytes 4732
  839.0 45.5 %copy-start.7 = (f32[394,768]{1,0:T(8,128)S(1)}, f32[394,768]{1,0:T(8,128)}, u32[]{:S(2)}) copy-start(f32[394,768]{1,0:T(8,128)} %copy-done.5) | copy-start | bytes 3631108
  839.0 45.5 %copy-start.89 = (f32[768]{0:T(1024)S(1)}, f32[768]{0:T(1024)}, u32[]{:S(2)}) copy-start(f32[768]{0:T(1024)} %copy-done.88) | copy-start | bytes 9220
  839.0 45.5 %copy-start.97 = (f32[394]{0:T(512)S(1)}, f32[394]{0:T(512)}, u32[]{:S(2)}) copy-start(f32[394]{0:T(512)} %copy-done.96) | copy-start | bytes 4732
  839.0 45.5 %copy-start.115 = (f32[394]{0:T(512)S(1)}, f32[394]{0:T(512)}, u32[]{:S(2)}) copy-start(f32[394]{0:T(512)} %copy-done.114) | copy-start | bytes 4732
  856.9 29.5 %copy-start.128 = (f32[394]{0:T(512)S(1)}, f32[394]{0:T(512)}, u32[]{:S(2)}) copy-start(f32[394]{0:T(512)} %copy-done.127) | copy-start | bytes 4732
  903.2 261.2 %all-reduce.26.cloned.1.call-start = ((), (), s32[]{:S(2)}) async-start(), calls=%async_computation.16 | async-start | bytes 18874368 | tf_op jit(solution)/shard_map/psum | solution.py:261
  914.9 270.3 %reduce-scatter.5.cloned.1.call-start = ((), (), s32[]{:S(2)}) async-start(), calls=%async_computation.15 | async-start | bytes 14155776 | tf_op jit(solution)/shard_map/reduce_scatter | solution.py:259
  927.3 279.9 %reduce-scatter.3.cloned.1.call-start = ((), (), s32[]{:S(2)}) async-start(), calls=%async_computation.14 | async-start | bytes 14155776 | tf_op jit(solution)/shard_map/reduce_scatter | solution.py:258
  941.6 34.5 %copy-start.126 = (f32[394]{0:T(512)S(1)}, f32[394]{0:T(512)}, u32[]{:S(2)}) copy-start(f32[394]{0:T(512)} %copy-done.125) | copy-start | bytes 4732
  974.3 67.9 %copy-start.10 = (f32[394,768]{1,0:T(8,128)S(1)}, f32[394,768]{1,0:T(8,128)}, u32[]{:S(2)}) copy-start(f32[394,768]{1,0:T(8,128)} %copy-done.8) | copy-start | bytes 3631108
  1164.3 42.9 %copy-start.61 = (f32[2,384,768]{2,1,0:T(8,128)S(1)}, f32[2,384,768]{2,1,0:T(8,128)}, u32[]{:S(2)}) copy-start(f32[2,384,768]{2,1,0:T(8,128)} %get-tuple-element.130) | copy-start | bytes 7077892
  (110 other events, 334.5 us)
Sparse Core Ops, SparseCore 0:
  21.8 46.6 all-reduce.13
  218.6 42.0 all-reduce.15
  272.3 43.9 all-reduce.17
  534.4 44.3 all-reduce.19
  634.8 43.1 all-reduce.21
  839.0 45.4 all-reduce.23
  903.3 70.9 all-reduce.27
  978.6 185.7 all-reduce.25
  1167.3 17.8 reduce-scatter.4
  1188.0 19.1 reduce-scatter.2
